TPU v7x, 256 devices: a whole 4x4x8 slice. The times are simulated.
256 devices in a mesh: row: 8 (over y_hi, x), col: 16 (over z, core), pole: 2 (over y_lo).
Axes of the slice: x: 4, y: 4 (y_hi: 2, y_lo: 2; y = y_hi * 2 + y_lo), z: 8, core: 2. Of those that a mesh axis runs over, the one named last changes fastest.
Arguments:
- inv_block: bfloat16 [2, 16384, 16384], P('pole', 'row', 'col'), may hold values from -6 to 6
- block_masks: int32 [2, 128, 128], P(None, 'row', 'col'), may hold values 0 or 1
- panel_first: bfloat16 [2, 16384, 512], P('pole', 'row'), may hold values from -0.046875 to 0.046875
- panel_second: bfloat16 [2, 16384, 512], P('pole', 'row'), may hold values from -0.046875 to 0.046875
- diag_inverse: bfloat16 [2, 2, 512, 512], P(None, 'pole'), may hold values from -6 to 6
- weights: float32 [2], P('pole'), may hold values from 0.3 to 1.2
Outputs:
- density_panels: bfloat16 [2, 16384, 512], P(None, ('row', 'col', 'pole'))
- density_diag: float32 [2, 512, 512], replicated
All inputs are finite; a program needn't handle non-finite values. No bound on the sum of `block_masks` on one device may be relied on, other than what follows from the above.
Results may differ from a plain program's by a relative error of at most 0.0043.
Values may be sent and summed in bfloat16 or wider, within the bound.
A program may use at most 64 MiB of HBM per device.

v0:
```python
import jax
import jax.numpy as jnp
from jax import lax
from jax.sharding import PartitionSpec as P


def from_root(block, axis, owner):
    block = jnp.where(lax.axis_index(axis) == owner, block, jnp.zeros_like(block))
    return lax.psum(block, axis)


def apply_mask(inverse, mask_rows):
    row_count, col_count = inverse.shape
    block_size = row_count // mask_rows.shape[0]
    shaped = inverse.reshape(mask_rows.shape[0], block_size, mask_rows.shape[1], block_size)
    mask_bf = mask_rows.astype(jnp.bfloat16)[:, None, :, None]
    return (shaped * mask_bf).reshape(row_count, col_count)


def local_partial(inverse, mask_rows, factor):
    col_count = inverse.shape[1]
    n_row = lax.axis_size("row")
    n_col = lax.axis_size("col")
    col_ratio = n_col // n_row
    col_idx = lax.axis_index("col")
    offset = col_idx % col_ratio * col_count
    factor_piece = lax.dynamic_slice_in_dim(factor, offset, col_count, 0)
    factor_cols = from_root(factor_piece, "row", col_idx // col_ratio)
    masked = apply_mask(inverse, mask_rows)
    return jnp.dot(masked, factor_cols, preferred_element_type=jnp.float32)


def panel_sum(partial_value, factor, diag_inv, weight):
    n_row = lax.axis_size("row")
    n_col = lax.axis_size("col")
    diag_share = diag_inv.astype(jnp.float32) / (n_row * n_col)
    summed = lax.psum_scatter(partial_value, "col", scatter_dimension=0, tiled=True)
    share_rows = summed.shape[0]
    factor_share = lax.dynamic_slice_in_dim(
        factor, lax.axis_index("col") * share_rows, share_rows, 0
    )
    inner_term = jnp.dot(
        factor_share.astype(jnp.float32).T, summed, precision=lax.Precision.HIGHEST
    )
    result = lax.psum_scatter(weight * summed, "pole", scatter_dimension=0, tiled=True)
    diag_term = weight * (diag_share - inner_term)
    return (result, diag_term)


def body(inv_block, block_masks, panel_first, panel_second, diag_inverse, weights):
    inverse = inv_block[0]
    weight = weights[0]
    partial_value = local_partial(inverse, block_masks[0], panel_first[0])
    dens_first, diag_term = panel_sum(partial_value, panel_first[0], diag_inverse[0, 0], weight)
    diag_first = lax.psum(diag_term, ("row", "col", "pole"))
    squares = lax.psum(jnp.sum(dens_first * dens_first, axis=0), ("row", "col", "pole"))
    total_rows = (
        dens_first.shape[0] * lax.axis_size("row") * lax.axis_size("col") * lax.axis_size("pole")
    )
    col_scale = jnp.sqrt(squares / total_rows + 1e-06)
    rescaled = (panel_second[0] / col_scale).astype(jnp.bfloat16)
    partial_second = local_partial(inverse, block_masks[1], rescaled)
    dens_second, diag_term_second = panel_sum(partial_second, rescaled, diag_inverse[1, 0], weight)
    diag_second = lax.psum(diag_term_second, ("row", "col", "pole"))
    density_panels = jnp.stack([dens_first, dens_second]).astype(jnp.bfloat16)
    density_diag = jnp.stack([diag_first, diag_second])
    return (density_panels, density_diag)


def solution(mesh):
    placed = (
        P("pole", "row", "col"),
        P(None, "row", "col"),
        P("pole", "row", None),
        P("pole", "row", None),
        P(None, "pole", None, None),
        P("pole"),
    )
    return jax.shard_map(
        body,
        mesh=mesh,
        in_specs=placed,
        out_specs=(P(None, ("row", "col", "pole"), None), P()),
        check_vma=False,
    )
```

profile of v0, /device:TPU:1, one launch (start us, length us, event | category | flops | bytes accessed | tf_op | source)
XLA Modules:
  0.0 732.8 jit_solution(13363967145291541522)
XLA Ops:
  7.2 0.0 all-reduce.5.cloned.1.call-start
  7.2 2.4 select_bitcast_fusion
  9.6 0.0 all-reduce.5.cloned.1.call-update
  9.6 0.0 reduce-scatter.5.cloned.1.call-start
  9.7 0.7 convert.13
  10.4 0.1 copy.8
  10.5 91.8 %all-reduce.5.cloned.1.call-done = bf16[1024,512]{1,0:T(8,128)(2,1)} async-done(((bf16[1024,512]{1,0:T(8,128)(2,1)}), bf16[1024,512]{1,0:T(8,128)(2,1)}) %all-reduce.5.cloned.1.call-update) | async-done | bytes 1048592 | tf_op jit(solution)/shard_map/psum | solution.py:9
  102.3 0.0 copy-start.2
  102.3 0.6 mul.54
  102.9 1.6 copy-done.2
  104.4 5.5 fusion.2
  110.0 0.0 reduce-scatter.5.cloned.1.call-update
  110.0 0.0 reduce-scatter.7.cloned.1.call-start
  110.7 63.4 %reduce-scatter.5.cloned.1.call-done = f32[128,512]{1,0:T(8,128)} async-done(((f32[2048,512]{1,0:T(8,128)}), f32[128,512]{1,0:T(8,128)}) %reduce-scatter.5.cloned.1.call-update) | async-done | bytes 262160 | tf_op jit(solution)/shard_map/reduce_scatter | solution.py:37
  174.1 1.7 broadcast_multiply_fusion.1
  175.8 0.0 reduce-scatter.7.cloned.1.call-update
  175.8 0.0 all-reduce.7.cloned.1.call-start
  175.8 19.6 %reduce-scatter.7.cloned.1.call-done = f32[64,512]{1,0:T(8,128)} async-done(((f32[128,512]{1,0:T(8,128)}), f32[64,512]{1,0:T(8,128)}) %reduce-scatter.7.cloned.1.call-update) | async-done | bytes 131088 | tf_op jit(solution)/shard_map/reduce_scatter | solution.py:45
  195.4 1.0 convert_bitcast_fusion.1
  196.5 77.0 %psum.36 = f32[512]{0:T(512)S(1)} all-reduce(f32[512]{0:T(512)S(1)} %get-tuple-element.5), channel_id=1, replica_groups=mesh['row'=8,'col'=16,'pole'=2] {'row','col','pole'}, use_global_device_ids=true, to_apply=%region_4.5 | all-reduce | flops 512 | bytes 4096 | tf_op jit(solution)/shard_map/psum | solution.py:56
  273.5 2.0 fusion.4
  275.5 1.2 dynamic-slice_select_fusion
  276.6 0.0 all-reduce.7.cloned.1.call-update
  276.7 0.0 reduce-scatter.9.cloned.1.call-start
  276.7 0.1 copy.9
  276.8 83.4 %all-reduce.7.cloned.1.call-done = bf16[1024,512]{1,0:T(8,128)(2,1)} async-done(((bf16[1024,512]{1,0:T(8,128)(2,1)}), bf16[1024,512]{1,0:T(8,128)(2,1)}) %all-reduce.7.cloned.1.call-update) | async-done | bytes 1048592 | tf_op jit(solution)/shard_map/psum | solution.py:9
  360.2 0.0 copy-start.3
  360.2 0.6 mul.59
  360.8 1.6 copy-done.3
  362.4 5.5 fusion
  367.9 0.0 copy-start
  367.9 0.0 copy-start.1
  367.9 0.0 reduce-scatter.9.cloned.1.call-update
  367.9 0.0 reduce-scatter.11.cloned.1.call-start
  368.0 64.2 %reduce-scatter.9.cloned.1.call-done = f32[128,512]{1,0:T(8,128)} async-done(((f32[2048,512]{1,0:T(8,128)}), f32[128,512]{1,0:T(8,128)}) %reduce-scatter.9.cloned.1.call-update) | async-done | bytes 262160 | tf_op jit(solution)/shard_map/reduce_scatter | solution.py:37
  432.2 1.7 broadcast_multiply_fusion
  433.9 0.0 reduce-scatter.11.cloned.1.call-update
  433.9 0.0 all-reduce.9.cloned.1.call-start
  434.0 0.0 copy-done
  434.0 0.0 copy-done.1
  434.0 2.6 fusion.10
  436.6 2.6 fusion.8
  439.2 0.0 all-reduce.9.cloned.1.call-update
  439.2 13.6 %reduce-scatter.11.cloned.1.call-done = f32[64,512]{1,0:T(8,128)} async-done(((f32[128,512]{1,0:T(8,128)}), f32[64,512]{1,0:T(8,128)}) %reduce-scatter.11.cloned.1.call-update) | async-done | bytes 131088 | tf_op jit(solution)/shard_map/reduce_scatter | solution.py:45
  452.9 0.9 convert_bitcast_fusion
  453.8 0.7 pad_maximum_fusion.1
  454.5 268.5 %all-reduce.9.cloned.1.call-done = (f32[1,512,512]{2,1,0:T(8,128)}, f32[1,512,512]{2,1,0:T(8,128)}) async-done(((f32[1,512,512]{2,1,0:T(8,128)}, f32[1,512,512]{2,1,0:T(8,128)}), (f32[1,512,512]{2,1,0:T(8,128)}, f32[1,512,512]{2,1,0:T(8,128)})) %all-reduce.9.cloned.1.call-update) | async-done | bytes 2097168 | tf_op jit(solution)/shard_map/psum | solution.py:64
  722.9 3.0 pad_maximum_fusion
  (2 shorter events, 0.0 us)
Async XLA Ops:
  7.2 95.1 %all-reduce.5.cloned.1.call-start = ((), (), s32[]{:S(2)}) async-start(), calls=%async_computation.4 | async-start | bytes 2097152 | tf_op jit(solution)/shard_map/psum | solution.py:9
  9.6 164.4 %reduce-scatter.5.cloned.1.call-start = ((), (), s32[]{:S(2)}) async-start(), calls=%async_computation.5 | async-start | bytes 4456448 | tf_op jit(solution)/shard_map/reduce_scatter | solution.py:37
  102.3 2.2 copy-start.2
  110.0 85.5 %reduce-scatter.7.cloned.1.call-start = ((), (), s32[]{:S(2)}) async-start(), calls=%async_computation.6 | async-start | bytes 393216 | tf_op jit(solution)/shard_map/reduce_scatter | solution.py:45
  175.8 184.4 %all-reduce.7.cloned.1.call-start = ((), (), s32[]{:S(2)}) async-start(), calls=%async_computation.7 | async-start | bytes 2097152 | tf_op jit(solution)/shard_map/psum | solution.py:9
  276.7 155.5 %reduce-scatter.9.cloned.1.call-start = ((), (), s32[]{:S(2)}) async-start(), calls=%async_computation.8 | async-start | bytes 4456448 | tf_op jit(solution)/shard_map/reduce_scatter | solution.py:37
  360.2 2.2 copy-start.3
  367.9 66.0 %copy-start = (bf16[2,1,512,512]{3,2,1,0:T(8,128)(2,1)S(1)}, bf16[2,1,512,512]{3,2,1,0:T(8,128)(2,1)}, u32[]{:S(2)}) copy-start(bf16[2,1,512,512]{3,2,1,0:T(8,128)(2,1)} %param.10) | copy-start | bytes 3145732
  367.9 66.1 %copy-start.1 = (f32[128,512]{1,0:T(8,128)S(1)}, f32[128,512]{1,0:T(8,128)}, u32[]{:S(2)}) copy-start(f32[128,512]{1,0:T(8,128)} %reduce-scatter.5.cloned.1.call-done) | copy-start | bytes 786436
  367.9 84.9 %reduce-scatter.11.cloned.1.call-start = ((), (), s32[]{:S(2)}) async-start(), calls=%async_computation.9 | async-start | bytes 393216 | tf_op jit(solution)/shard_map/reduce_scatter | solution.py:45
  433.9 289.0 %all-reduce.9.cloned.1.call-start = ((), (), s32[]{:S(2)}) async-start(), calls=%async_computation.10 | async-start | bytes 4194304 | tf_op jit(solution)/shard_map/psum | solution.py:64
Sparse Core Ops, SparseCore 0:
  11.2 91.0 all-reduce.4
  110.1 63.9 reduce-scatter.4
  177.1 18.2 reduce-scatter.6
  276.8 83.3 all-reduce.6
  368.1 64.1 reduce-scatter.8
  434.5 18.2 reduce-scatter.10
  459.0 263.8 all-reduce.8
where the time goes:
time: 734 us; the launch traced here: 733 us
  waiting for transfers between devices  605 us (82%)
  blocking collectives  77 us (10%)
  matrix products  16.3 us (2%)
  other arithmetic  15.2 us (2%)
  between operations  14.8 us (2%)
    psum x1, waiting for transfers between devices, body(): diag_second = lax.psum(diag_term_second, ('row', 'col', 'pole'))  268 us
    psum x2, waiting for transfers between devices, from_root(): return lax.psum(block, axis)  175 us
    reduce_scatter x2, waiting for transfers between devices, panel_sum(): lax.psum_scatter(partial_value, 'col', scatter_dimension=0, tiled=True)  128 us
    psum x1, blocking collectives, body(): lax.psum(jnp.sum(dens_first * dens_first, axis=0), ('row', 'col', 'pole'))  77 us
    reduce_scatter x2, waiting for transfers between devices, panel_sum(): lax.psum_scatter(weight * summed, 'pole', scatter_dimension=0, tiled=True)  33.2 us
  transfers between devices with their start and end apart: 7, of which 7 were waited for; matrix products, arithmetic and copies ran while one was open for 1% of the time, Pallas kernels for 0%

commit v1 on v0

v1 whole, which is shorter than its diff:
```python
import jax
import jax.numpy as jnp
from jax import lax
from jax.experimental import pallas as pl
from jax.experimental.pallas import tpu as pltpu
from jax.sharding import PartitionSpec as P

MESH = pl.DeviceIdType.MESH
F32 = jnp.float32
BF16 = jnp.bfloat16

UNITS = 4
SUBS = 4
OFFSETS = (4, 3, 5, 2, 6, 1, 7, 0)
PLUS = (0, 1, 3, 5)
MINUS = (0, 2, 4, 6)


def rem(a, n):
    return lax.rem(a, jnp.int32(n))


def div(a, n):
    return lax.div(a, jnp.int32(n))


def kernel(
    inv_hbm, mask_ref, p0_hbm, p1_hbm, diag_hbm, w_ref,
    dens_out, diag_out,
    inv, masked, fac, relay, pan, pan_t, part, acc, xr, zs, zr, fin, ps, pr,
    dens, e_acc, es, er1, eq, er2, e3, e4, dg, dslice, dsum, dps, dpr,
    sq1, sq1r, sq2, sq3,
    load_sem, diag_sem,
    root_send, rb_recv, ax_send, ay_send, f_recv,
    x_send, x_recv, z_send, z_recv, p_send, p_recv,
    e1_send, e1_recv, e2_send, e2_recv, e3_send, e3_recv, e4_send, e4_recv, e5_send, e5_recv,
    s1_send, s1_recv, s2_send, s2_recv, s3_send, s3_recv, d_send, d_recv,
):
    row = lax.axis_index("row")
    col = lax.axis_index("col")
    p = lax.axis_index("pole")
    x, yh = rem(row, 4), div(row, 4)
    z, o = div(col, 2), rem(col, 2)
    y = yh * 2 + p
    xroot, yroot_h = rem(z, 4), div(z, 4)
    dx = rem(x - xroot + 4, 4)
    dy = rem(y - (yroot_h * 2 + 1 - p) + 8, 4)
    half = div(dy, 2)
    is_root = jnp.logical_and(dx == 0, yh == yroot_h)
    q = y * 4 + x

    def dev(x_, y_, z_, o_):
        return {"row": div(y_, 2) * 4 + x_, "col": z_ * 2 + o_, "pole": rem(y_, 2)}

    xp, xm = rem(x + 1, 4), rem(x + 3, 4)
    yp, ym = rem(y + 1, 4), rem(y + 3, 4)
    zp, zm = rem(z + 1, 8), rem(z + 7, 8)
    d_core = dev(x, y, z, 1 - o)
    d_xp, d_xm = dev(xp, y, z, o), dev(xm, y, z, o)
    d_yp, d_ym = dev(x, yp, z, o), dev(x, ym, z, o)
    d_zp, d_zm = dev(x, y, zp, o), dev(x, y, zm, o)
    d_pole = dev(x, yh * 2 + 1 - p, z, o)

    def plane(d):
        t = rem(q + d, 16)
        return dev(rem(t, 4), div(t, 4), z, o)

    def along(d):
        return dev(x, y, rem(z + d, 8), o)

    def rcopy(src, dst, ssem, rsem, to):
        return pltpu.make_async_remote_copy(
            src_ref=src, dst_ref=dst, send_sem=ssem, recv_sem=rsem, device_id=to, device_id_type=MESH
        )

    barrier = pltpu.get_barrier_semaphore()
    pl.semaphore_signal(barrier, inc=1, device_id=d_core, device_id_type=MESH)

    @pl.loop(1, 16)
    def _(d):
        pl.semaphore_signal(barrier, inc=1, device_id=plane(d), device_id_type=MESH)

    @pl.loop(1, 8)
    def _(d):
        pl.semaphore_signal(barrier, inc=1, device_id=along(d), device_id_type=MESH)

    ld_inv = pltpu.make_async_copy(inv_hbm.at[0], inv, load_sem.at[0])
    ld_p0 = pltpu.make_async_copy(p0_hbm.at[0], pan.at[0], load_sem.at[1])
    ld_p1 = pltpu.make_async_copy(p1_hbm.at[0], pan.at[1], load_sem.at[2])
    q_pole = (yh * 2 + 1 - p) * 4 + x
    ld_diag = []
    for k in range(2):
        for s, who in enumerate((q, q_pole)):
            at = pl.multiple_of(o * 256 + who * 16, 16)
            ld_diag.append(
                pltpu.make_async_copy(diag_hbm.at[k, 0, pl.ds(at, 16), :], dslice.at[k, s], diag_sem.at[k, s])
            )
    ld_inv.start()
    ld_p0.start()
    ld_p1.start()
    for c in ld_diag:
        c.start()

    w = w_ref[0]

    pl.semaphore_wait(barrier, 23)

    def root_copies(u, i):
        k, n = divmod(u, 2)
        panel = (p0_hbm, p1_hbm)[k]
        out = []
        for hf, to in ((0, d_yp), (1, d_ym)):
            at = pl.multiple_of(o * 1024 + hf * 512 + i * 128, 128)
            src = panel.at[0, pl.ds(at, 128), pl.ds(n * 256, 256)]
            out.append(rcopy(src, relay.at[u, i], root_send.at[u, i, hf], rb_recv.at[u, i], to))
        return out

    @pl.when(is_root)
    def _():
        for u in range(UNITS):
            for i in range(SUBS):
                for c in root_copies(u, i):
                    c.start()

    def y_copies(u, i):
        slot = half * SUBS + i
        return [
            rcopy(relay.at[u, i], fac.at[u, slot], ay_send.at[u, i, s], f_recv.at[u, slot], to)
            for s, to in ((0, d_yp), (1, d_ym))
        ]

    def x_copies(u, i):
        plus = rcopy(relay.at[u, i], relay.at[u, i], ax_send.at[u, i, 0], rb_recv.at[u, i], d_xp)
        minus = rcopy(relay.at[u, i], relay.at[u, i], ax_send.at[u, i, 1], rb_recv.at[u, i], d_xm)
        first = dx == 0
        if i % 2 == 0:
            return ((jnp.logical_or(first, dx == 1), plus), (first, minus))
        return ((first, plus), (jnp.logical_or(first, dx == 3), minus))

    def forward(u, i):
        rcopy(relay.at[u, i], relay.at[u, i], ax_send.at[u, i, 0], rb_recv.at[u, i], d_xp).wait_recv()
        for cond, c in x_copies(u, i):
            pl.when(cond)(c.start)
        for c in y_copies(u, i):
            c.start()

    def apply_masks(k):
        @pl.loop(0, 16)
        def _(i):
            rows = pl.ds(pl.multiple_of(i * 128, 128), 128)
            for j in range(8):
                m = jnp.full((16, 128), mask_ref[k, i, j].astype(F32), F32).astype(BF16)
                blk = inv[rows, pl.ds(j * 128, 128)].reshape(8, 16, 128)
                masked[k, rows, pl.ds(j * 128, 128)] = (blk * m[None]).reshape(128, 128)

    def transpose_panel(k):
        @pl.loop(0, 8)
        def _(i):
            at = pl.multiple_of(i * 256, 256)
            pan_t[k, :, pl.ds(at, 256)] = pan[k, pl.ds(at, 256), :].T

    def x_copy(u, j):
        zt = rem(z + OFFSETS[j], 8) if isinstance(j, int) else None
        at = pl.multiple_of(zt * 256 + (1 - o) * 128, 128)
        return rcopy(part.at[u, pl.ds(at, 128), :], xr.at[u, j], x_send.at[u, j], x_recv.at[u, j], d_core)

    def wait_factor(u):
        for slot in range(2 * SUBS):
            rcopy(relay.at[u, 0], fac.at[u, slot], ay_send.at[u, 0, 0], f_recv.at[u, slot], d_yp).wait_recv()

    def multiply(u, g):
        k = u // 2
        for j in (2 * g, 2 * g + 1):
            zt = rem(z + OFFSETS[j], 8)
            rows = pl.ds(pl.multiple_of(zt * 256, 256), 256)
            val = jnp.dot(masked[k, rows, :], fac[u].reshape(1024, 256), preferred_element_type=F32) * w
            acc[u, j] = val
            part[u, rows, :] = val.astype(BF16)
            x_copy(u, j).start()

    def inner(u):
        k, n = divmod(u, 2)

        @pl.loop(0, 2)
        def _(i):
            rows = pl.ds(pl.multiple_of(i * 256, 256), 256)
            e_acc[k, rows, pl.ds(n * 256, 256)] = jnp.dot(
                pan_t[k, rows, :], part[u], preferred_element_type=F32
            )

    def z_copy(u, d, s):
        to = (d_zp, d_zm)[d]
        rows = pl.ds(0, 64) if s == 0 else pl.ds(0, 128)
        return rcopy(
            zs.at[u, d, s, rows, :], zr.at[u, d, s, rows, :], z_send.at[u, d, s], z_recv.at[u, d, s], to
        )

    def own(u, j):
        x_copy(u, j).wait_recv()
        at = pl.multiple_of(o * 128, 128)
        return acc[u, j, pl.ds(at, 128), :] + xr[u, j].astype(F32)

    def ring(u, s):
        if s == 0:
            val = own(u, 0).astype(BF16)
            zs[u, 0, 0, 0:64, :] = val[0:64]
            zs[u, 1, 0, 0:64, :] = val[64:128]
            z_copy(u, 0, 0).start()
            z_copy(u, 1, 0).start()
            return
        for d, js in ((0, PLUS), (1, MINUS)):
            val = own(u, js[s])
            z_copy(u, d, s - 1).wait_recv()
            if s == 1:
                lo, hi = val[0:64], val[64:128]
                got = zr[u, d, 0, 0:64, :].astype(F32)
                if d == 0:
                    lo = lo + got
                else:
                    hi = hi + got
                zs[u, d, 1, 0:64, :] = lo.astype(BF16)
                zs[u, d, 1, 64:128, :] = hi.astype(BF16)
            else:
                zs[u, d, s] = (val + zr[u, d, s - 1].astype(F32)).astype(BF16)
            z_copy(u, d, s).start()

    def pole_copy(u):
        return rcopy(ps.at[u], pr.at[u], p_send.at[u], p_recv.at[u], d_pole)

    def finish(u):
        val = own(u, 7)
        z_copy(u, 0, 3).wait_recv()
        z_copy(u, 1, 3).wait_recv()
        fin[u] = val + zr[u, 0, 3].astype(F32) + zr[u, 1, 3].astype(F32)
        ps[u] = fin[u, pl.ds(pl.multiple_of((1 - p) * 64, 64), 64), :].astype(BF16)
        pole_copy(u).start()

    def pole_sum(u):
        k, n = divmod(u, 2)
        pole_copy(u).wait_recv()
        val = fin[u, pl.ds(pl.multiple_of(p * 64, 64), 64), :] + pr[u].astype(F32)
        dens[k, :, pl.ds(n * 256, 256)] = val

    def s1_copy():
        return rcopy(sq1, sq1r, s1_send.at[0], s1_recv.at[0], d_core)

    def s2_copy(d):
        return rcopy(sq2.at[z], sq2.at[z], s2_send.at[d], s2_recv.at[d], along(d))

    def s3_copy(d):
        return rcopy(sq3.at[q], sq3.at[q], s3_send.at[d], s3_recv.at[d], plane(d))

    def squares1():
        sq1[...] = jnp.zeros_like(sq1)
        for c in range(4):
            v = dens[0, :, pl.ds(c * 128, 128)]
            sq1[c : c + 1, :] = jnp.sum(v * v, axis=0, keepdims=True)
        s1_copy().start()

    def squares2():
        s1_copy().wait_recv()
        sq2[z] = sq1[...] + sq1r[...]

        @pl.loop(1, 8)
        def _(d):
            s2_copy(d).start()

    def squares3():
        @pl.loop(1, 8)
        def _(d):
            s2_copy(d).wait_recv()

        tot = sq2[0]
        for i in range(1, 8):
            tot = tot + sq2[i]
        sq3[q] = tot

        @pl.loop(1, 16)
        def _(d):
            s3_copy(d).start()

    def squares4():
        @pl.loop(1, 16)
        def _(d):
            s3_copy(d).wait_recv()

        tot = sq3[0]
        for i in range(1, 16):
            tot = tot + sq3[i]
        sq1r[...] = jnp.sqrt(tot * (1.0 / 16384.0) + 1e-6)

    def scale_row():
        return jnp.concatenate([sq1r[c : c + 1, :] for c in range(4)], axis=1)

    def d_copy(k):
        return rcopy(dps.at[k], dpr.at[k], d_send.at[k], d_recv.at[k], d_pole)

    def diag_exchange():
        for c in ld_diag:
            c.wait()
        for k in range(2):
            dsum[k] = dslice[k, 0].astype(F32) * w
            dps[k] = dslice[k, 1].astype(F32) * w
            d_copy(k).start()

    def e1_copy(k):
        return rcopy(es.at[k], er1.at[k], e1_send.at[k], e1_recv.at[k], d_core)

    def e2_copy(k, d):
        t = rem(q + d, 16)
        return rcopy(eq.at[k, t], er2.at[k, d], e2_send.at[k, d], e2_recv.at[k, d], plane(d))

    def e3_copy(k, d):
        return rcopy(e3.at[k, z], e3.at[k, z], e3_send.at[k, d], e3_recv.at[k, d], along(d))

    def e4_copy(k, d):
        return rcopy(e4.at[k], dg.at[k, o, q], e4_send.at[k, d], e4_recv.at[k, d], plane(d))

    def e5_copy(k):
        return rcopy(dg.at[k, o], dg.at[k, o], e5_send.at[k], e5_recv.at[k], d_core)

    def diag1(k):
        at = pl.multiple_of((1 - o) * 256, 256)
        es[k] = e_acc[k, pl.ds(at, 256), :].astype(BF16)
        e1_copy(k).start()

    def diag2(k):
        e1_copy(k).wait_recv()

        @pl.loop(0, 16)
        def _(t):
            at = pl.multiple_of(o * 256 + t * 16, 16)
            r = pl.ds(pl.multiple_of(t * 16, 16), 16)
            eq[k, t] = (e_acc[k, pl.ds(at, 16), :] + er1[k, r, :].astype(F32)).astype(BF16)

        @pl.loop(1, 16)
        def _(d):
            e2_copy(k, d).start()

    def diag3(k):
        @pl.loop(1, 16)
        def _(d):
            e2_copy(k, d).wait_recv()

        tot = eq[k, q].astype(F32)
        for i in range(1, 16):
            tot = tot + er2[k, i].astype(F32)
        e3[k, z] = tot.astype(BF16)

        @pl.loop(1, 8)
        def _(d):
            e3_copy(k, d).start()

    def diag4(k):
        @pl.loop(1, 8)
        def _(d):
            e3_copy(k, d).wait_recv()

        tot = e3[k, 0].astype(F32)
        for i in range(1, 8):
            tot = tot + e3[k, i].astype(F32)
        if k == 1:
            s = scale_row()
            base = o * 256 + q * 16
            ri = lax.broadcasted_iota(jnp.int32, (16, 512), 0) + base
            ci = lax.broadcasted_iota(jnp.int32, (16, 512), 1)
            s_full = jnp.broadcast_to(s, (16, 512))
            s_col = jnp.sum(jnp.where(ri == ci, s_full, 0.0), axis=1, keepdims=True)
            tot = tot / s_full / s_col
        d_copy(k).wait_recv()
        both = jnp.where(p == 0, dsum[k] + dpr[k], dpr[k] + dsum[k])
        val = (both - tot).astype(BF16)
        e4[k] = val
        dg[k, o, q] = val

        @pl.loop(1, 16)
        def _(d):
            e4_copy(k, d).start()

    def diag5(k):
        @pl.loop(1, 16)
        def _(d):
            e4_copy(k, d).wait_recv()

        e5_copy(k).start()

    def diag6(k):
        e5_copy(k).wait_recv()

    ld_inv.wait()
    apply_masks(0)
    for i in range(SUBS):
        forward(0, i)
    apply_masks(1)
    diag_exchange()
    for u in range(UNITS):
        if u < 3:
            forward(u + 1, 0)
        wait_factor(u)
        for g in range(4):
            multiply(u, g)
            if u < 3 and g < 3:
                forward(u + 1, g + 1)
        ring(u, 0)
        if u >= 1:
            ring(u - 1, 1)
        if u >= 2:
            ring(u - 2, 2)
        if u >= 3:
            ring(u - 3, 3)
        if u == 0:
            ld_p0.wait()
            transpose_panel(0)
        if u == 2:
            ld_p1.wait()
            transpose_panel(1)
        inner(u)
        if u == 1:
            diag1(0)
        if u == 2:
            diag2(0)
        if u == 3:
            diag1(1)
            diag3(0)
    ring(3, 1)
    ring(2, 2)
    ring(1, 3)
    finish(0)
    diag2(1)
    ring(3, 2)
    ring(2, 3)
    finish(1)
    pole_sum(0)
    ring(3, 3)
    pole_sum(1)
    squares1()
    diag4(0)
    finish(2)
    squares2()
    diag3(1)
    finish(3)
    pole_sum(2)
    squares3()
    diag5(0)
    pole_sum(3)
    squares4()
    diag4(1)
    dens_out[0] = dens[0].astype(BF16)
    dens_out[1] = (dens[1] / scale_row()).astype(BF16)
    diag6(0)
    diag5(1)
    diag6(1)
    diag_out[...] = dg[...]

    @pl.when(is_root)
    def _():
        for u in range(UNITS):
            for i in range(SUBS):
                for c in root_copies(u, i):
                    c.wait_send()

    for u in range(UNITS):
        for i in range(SUBS):
            for cond, c in x_copies(u, i):
                pl.when(cond)(c.wait_send)
            for c in y_copies(u, i):
                c.wait_send()
        for j in range(8):
            x_copy(u, j).wait_send()
        for d in range(2):
            for s in range(4):
                z_copy(u, d, s).wait_send()
        pole_copy(u).wait_send()
    s1_copy().wait_send()

    @pl.loop(1, 8)
    def _(d):
        s2_copy(d).wait_send()
        e3_copy(0, d).wait_send()
        e3_copy(1, d).wait_send()

    @pl.loop(1, 16)
    def _(d):
        s3_copy(d).wait_send()
        for k in range(2):
            e2_copy(k, d).wait_send()
            e4_copy(k, d).wait_send()

    for k in range(2):
        d_copy(k).wait_send()
        e1_copy(k).wait_send()
        e5_copy(k).wait_send()


def body(inv_block, block_masks, panel_first, panel_second, diag_inverse, weights):
    vmem = pltpu.VMEM
    dma = pltpu.SemaphoreType.DMA
    any_spec = pl.BlockSpec(memory_space=pl.ANY)
    smem = pl.BlockSpec(memory_space=pltpu.SMEM)
    out_vmem = pl.BlockSpec(memory_space=pltpu.VMEM)
    scratch = [
        vmem((2048, 1024), BF16),
        vmem((2, 2048, 1024), BF16),
        vmem((UNITS, 2 * SUBS, 128, 256), BF16),
        vmem((UNITS, SUBS, 128, 256), BF16),
        vmem((2, 2048, 512), BF16),
        vmem((2, 512, 2048), BF16),
        vmem((UNITS, 2048, 256), BF16),
        vmem((UNITS, 8, 256, 256), F32),
        vmem((UNITS, 8, 128, 256), BF16),
        vmem((UNITS, 2, 4, 128, 256), BF16),
        vmem((UNITS, 2, 4, 128, 256), BF16),
        vmem((UNITS, 128, 256), F32),
        vmem((UNITS, 64, 256), BF16),
        vmem((UNITS, 64, 256), BF16),
        vmem((2, 64, 512), F32),
        vmem((2, 512, 512), F32),
        vmem((2, 256, 512), BF16),
        vmem((2, 256, 512), BF16),
        vmem((2, 16, 16, 512), BF16),
        vmem((2, 16, 16, 512), BF16),
        vmem((2, 8, 16, 512), BF16),
        vmem((2, 16, 512), BF16),
        vmem((2, 2, 16, 16, 512), BF16),
        vmem((2, 2, 16, 512), BF16),
        vmem((2, 16, 512), F32),
        vmem((2, 16, 512), F32),
        vmem((2, 16, 512), F32),
        vmem((8, 128), F32),
        vmem((8, 128), F32),
        vmem((8, 8, 128), F32),
        vmem((16, 8, 128), F32),
        dma((3,)),
        dma((2, 2)),
        dma((UNITS, SUBS, 2)),
        dma((UNITS, SUBS)),
        dma((UNITS, SUBS, 2)),
        dma((UNITS, SUBS, 2)),
        dma((UNITS, 2 * SUBS)),
        dma((UNITS, 8)),
        dma((UNITS, 8)),
        dma((UNITS, 2, 4)),
        dma((UNITS, 2, 4)),
        dma((UNITS,)),
        dma((UNITS,)),
        dma((2,)),
        dma((2,)),
        dma((2, 16)),
        dma((2, 16)),
        dma((2, 8)),
        dma((2, 8)),
        dma((2, 16)),
        dma((2, 16)),
        dma((2,)),
        dma((2,)),
        dma((1,)),
        dma((1,)),
        dma((8,)),
        dma((8,)),
        dma((16,)),
        dma((16,)),
        dma((2,)),
        dma((2,)),
    ]
    dens, diag = pl.pallas_call(
        kernel,
        out_shape=(
            jax.ShapeDtypeStruct((2, 64, 512), BF16),
            jax.ShapeDtypeStruct((2, 2, 16, 16, 512), BF16),
        ),
        in_specs=[any_spec, smem, any_spec, any_spec, any_spec, smem],
        out_specs=(out_vmem, out_vmem),
        scratch_shapes=scratch,
        compiler_params=pltpu.CompilerParams(
            collective_id=0, has_side_effects=True, vmem_limit_bytes=60 * 1024 * 1024
        ),
    )(inv_block, block_masks, panel_first, panel_second, diag_inverse, weights)
    return dens, diag.reshape(2, 512, 512).astype(F32)


def solution(mesh):
    placed = (
        P("pole", "row", "col"),
        P(None, "row", "col"),
        P("pole", "row", None),
        P("pole", "row", None),
        P(None, "pole", None, None),
        P("pole"),
    )
    return jax.shard_map(
        body,
        mesh=mesh,
        in_specs=placed,
        out_specs=(P(None, ("row", "col", "pole"), None), P()),
        check_vma=False,
    )
```

time: 734 us -> 123 us (0.17)
  waiting for transfers between devices: 605 us -> 0 us
  Pallas kernels: 0 us -> 117 us
  blocking collectives: 77 us -> 0 us
  matrix products: 16.3 us -> 0 us
  between operations: 14.8 us -> 1.29 us
  other arithmetic: 15.2 us -> 2.87 us
    psum x3 -> x0, waiting for transfers between devices: 444 us -> none  [the longest x1 268 us: body(): diag_second = lax.psum(diag_term_second, ('row', 'col', 'pole'))]
    reduce_scatter x4 -> x0, waiting for transfers between devices: 161 us -> none  [the longest x2 128 us: panel_sum(): lax.psum_scatter(partial_value, 'col', scatter_dimension=0, tiled=True)]
    pallas_call x0 -> x1, Pallas kernels: none -> 117 us  [body(): pl.pallas_call(kernel, out_shape=(jax.ShapeDtypeStruct((2, 64, 512), BF16...]
    psum x1 -> x0, blocking collectives: 77 us -> none  [body(): lax.psum(jnp.sum(dens_first * dens_first, axis=0), ('row', 'col', 'pole'))]
    dot_general x4 -> x0, matrix products: 16.3 us -> none  [the longest x2 11 us: local_partial(): return jnp.dot(masked, factor_cols, preferred_element_type=jnp.float32)]
  transfers between devices with their start and end apart: 7 -> 0, of which waited for: 7 -> 0; matrix products, arithmetic and copies ran while one was open for 1% -> 0% of each run, Pallas kernels for 0% -> 0%
where the time goes in v1:
time: 123 us
  Pallas kernels  117 us (95%)
  other arithmetic  2.87 us (2%)
  local copies, waits for them, and re-layouts  2.04 us (2%)
  between operations  1.29 us (1%)
    pallas_call x1, Pallas kernels, body(): pl.pallas_call(kernel, out_shape=(jax.ShapeDtypeStruct((2, 64, 512), BF16...  117 us
    convert_element_type x1, other arithmetic, body(): return (dens, diag.reshape(2, 512, 512).astype(F32))  2.87 us

profile of v1, /device:TPU:1, one launch (start us, length us, event | category | flops | bytes accessed | tf_op | source)
XLA Modules:
  0.0 123.3 jit_solution(10757283799222420979)
XLA Ops:
  1.3 1.4 %copy.8.mask_ref = s32[2,16,8]{2,1,0:T(8,128)} copy(s32[2,16,8]{1,2,0:T(8,128)} %param.7) | data formatting | bytes 2048 | tf_op args[1]
  2.7 117.1 %shard_map.77 = (bf16[2,64,512]{2,1,0:T(8,128)(2,1)}, bf16[2,2,16,16,512]{4,3,2,1,0:T(8,128)(2,1)}) custom-call(bf16[1,2048,1024]{2,1,0:T(8,128)(2,1)} %inv_hbm.1, s32[2,16,8]{2,1,0:T(8,128)} %copy.8.mask_ref, bf16[1,2048,512]{2,1,0:T(8,128)(2,1)} %p0_hbm.1, bf16[1,2048,512]{2,1,0:T(8,128)(2,1)} %p1_hbm.1, bf16[2,1,512,512]{3,2,1,0:T(8,128)(2,1)} %diag_hbm.1, ...), custom_call_target="tpu_custom_call" | custom-call | tf_op jit(solution)/shard_map/pallas_call | solution.py:565
  119.7 0.0 copy-start
  119.7 2.9 %bitcast_convert_fusion = f32[2,512,512]{2,1,0:T(8,128)} fusion(bf16[2,2,16,16,512]{4,3,2,1,0:T(8,128)(2,1)} %get-tuple-element.5), kind=kLoop, calls=%fused_computation | loop fusion | flops 524288 | bytes 3145728 | tf_op jit(solution)/shard_map/convert_element_type | solution.py:578
  122.6 0.0 copy-done
  122.6 0.7 copy.11
Async XLA Ops:
  119.7 2.9 %copy-start = (bf16[2,64,512]{2,1,0:T(8,128)(2,1)S(1)}, bf16[2,64,512]{2,1,0:T(8,128)(2,1)}, u32[]{:S(2)}) copy-start(bf16[2,64,512]{2,1,0:T(8,128)(2,1)} %get-tuple-element.8) | copy-start | bytes 393220

commit v2 on v1

v2 whole, which is shorter than its diff:
```python
import jax
import jax.numpy as jnp
from jax import lax
from jax.experimental import pallas as pl
from jax.experimental.pallas import tpu as pltpu
from jax.sharding import PartitionSpec as P

MESH = pl.DeviceIdType.MESH
F32 = jnp.float32
BF16 = jnp.bfloat16

UNITS = 4
SUBS = 4
ROWS = 512 // SUBS
AHEAD = 8
LEAD_FIRST = 10
LEAD_REST = 5
OFFSETS = (4, 3, 5, 2, 6, 1, 7, 0)
PLUS = (0, 1, 3, 5)
MINUS = (0, 2, 4, 6)


def rem(a, n):
    return lax.rem(a, jnp.int32(n))


def div(a, n):
    return lax.div(a, jnp.int32(n))


def kernel(
    inv_hbm, mask_ref, p0_hbm, p1_hbm, diag_hbm, w_ref,
    dens_out, diag_out,
    inv, masked, fac, relay, pan, pan_t, part, acc, xr, zs, zr, fin, pr,
    dens, e_acc, es, er1, eq, er2, e3, e4, dg, dslice, dsum, dps, dpr,
    scale, sq2, sq3,
    here, load_sem, diag_sem,
    root_send, rb_recv, ax_send, ay_send, fill_send, f_recv,
    x_send, x_recv, z_send, z_recv, p_send, p_recv,
    e1_send, e1_recv, e2_send, e2_recv, e3_send, e3_recv, e4_send, e4_recv, e5_send, e5_recv,
    s2_send, s2_recv, s3_send, s3_recv, d_send, d_recv,
):
    row = lax.axis_index("row")
    col = lax.axis_index("col")
    p = lax.axis_index("pole")
    x, yh = rem(row, 4), div(row, 4)
    z, o = div(col, 2), rem(col, 2)
    y = yh * 2 + p
    xroot, yroot_h = rem(z, 4), div(z, 4)
    dx = rem(x - xroot + 4, 4)
    dy = rem(y - (yroot_h * 2 + 1 - p) + 8, 4)
    half = div(dy, 2)
    is_root = jnp.logical_and(dx == 0, yh == yroot_h)
    q = y * 4 + x

    def dev(x_, y_, z_, o_):
        return {"row": div(y_, 2) * 4 + x_, "col": z_ * 2 + o_, "pole": rem(y_, 2)}

    xp, xm = rem(x + 1, 4), rem(x + 3, 4)
    yp, ym = rem(y + 1, 4), rem(y + 3, 4)
    zp, zm = rem(z + 1, 8), rem(z + 7, 8)
    d_core = dev(x, y, z, 1 - o)
    d_xp, d_xm = dev(xp, y, z, o), dev(xm, y, z, o)
    d_yp, d_ym = dev(x, yp, z, o), dev(x, ym, z, o)
    d_zp, d_zm = dev(x, y, zp, o), dev(x, y, zm, o)
    d_pole = dev(x, yh * 2 + 1 - p, z, o)

    def plane(d):
        t = rem(q + d, 16)
        return dev(rem(t, 4), div(t, 4), z, o)

    def along(d):
        return dev(x, y, rem(z + d, 8), o)

    def rcopy(src, dst, ssem, rsem, to):
        return pltpu.make_async_remote_copy(
            src_ref=src, dst_ref=dst, send_sem=ssem, recv_sem=rsem, device_id=to, device_id_type=MESH
        )

    sent = []

    def send(make):
        make().start()
        sent.append(lambda: make().wait_send())

    def send_if(cond, make):
        pl.when(cond)(lambda: make().start())
        sent.append(lambda: pl.when(cond)(lambda: make().wait_send()))

    def send_all(make, n):
        pl.loop(1, n)(lambda d: make(d).start())
        sent.append(lambda: pl.loop(1, n)(lambda d: make(d).wait_send()))

    barrier = pltpu.get_barrier_semaphore()
    for to in (d_core, d_xp, d_xm, d_yp, d_ym, d_zp, d_zm):
        pl.semaphore_signal(barrier, inc=1, device_id=to, device_id_type=MESH)

    ld_inv = pltpu.make_async_copy(inv_hbm.at[0], inv, load_sem.at[0])
    ld_p0 = pltpu.make_async_copy(p0_hbm.at[0], pan.at[0], load_sem.at[1])
    ld_p1 = pltpu.make_async_copy(p1_hbm.at[0], pan.at[1], load_sem.at[2])
    q_pole = (yh * 2 + 1 - p) * 4 + x
    ld_diag = []
    for k in range(2):
        for s, who in enumerate((q, q_pole)):
            at = pl.multiple_of(o * 256 + who * 16, 16)
            ld_diag.append(
                pltpu.make_async_copy(diag_hbm.at[k, 0, pl.ds(at, 16), :], dslice.at[k, s], diag_sem.at[k, s])
            )
    ld_inv.start()
    ld_p0.start()
    ld_p1.start()
    for c in ld_diag:
        c.start()

    w = w_ref[0]

    pl.semaphore_wait(barrier, 7)

    def tell(i, *to):
        for d in to:
            pl.semaphore_signal(here.at[i], inc=1, device_id=d, device_id_type=MESH)

    def told(i):
        pl.semaphore_wait(here.at[i], 2)

    def root_copies(u, i):
        k, n = divmod(u, 2)
        panel = (p0_hbm, p1_hbm)[k]
        out = []
        for hf, to in ((0, d_yp), (1, d_ym)):
            at = pl.multiple_of(o * 1024 + hf * 512 + i * ROWS, ROWS)
            src = panel.at[0, pl.ds(at, ROWS), pl.ds(n * 256, 256)]
            out.append(rcopy(src, relay.at[u, i], root_send.at[u, i, hf], rb_recv.at[u, i], to))
        return out

    def root_start(u, i):
        for h in range(2):
            send_if(is_root, lambda h=h: root_copies(u, i)[h])

    def y_copies(u, i):
        slot = half * SUBS + i
        return [
            rcopy(relay.at[u, i], fac.at[u, slot], ay_send.at[u, i, s], f_recv.at[u, slot], to)
            for s, to in ((0, d_yp), (1, d_ym))
        ]

    def x_copy_to(u, i, h):
        to = (d_xp, d_xm)[h]
        return rcopy(relay.at[u, i], relay.at[u, i], ax_send.at[u, i, h], rb_recv.at[u, i], to)

    first = dx == 0

    def forward_first(n):
        if n >= UNITS * SUBS:
            return
        u, i = divmod(n, SUBS)
        if n + AHEAD < UNITS * SUBS:
            root_start(*divmod(n + AHEAD, SUBS))
        pl.when(first)(lambda: x_copy_to(u, i, 0).wait_recv())
        for h in range(2):
            send_if(first, lambda h=h: x_copy_to(u, i, h))

    def forward_rest(n):
        if n >= UNITS * SUBS:
            return
        u, i = divmod(n, SUBS)
        h = i % 2
        pl.when(dx != 0)(lambda: x_copy_to(u, i, 0).wait_recv())
        send_if(dx == (3 if h else 1), lambda: x_copy_to(u, i, h))
        for s in range(2):
            send_if(dx != 0, lambda s=s: y_copies(u, i)[s])

    done = [0, 0]

    def forward(t):
        t = t * SUBS // 4
        while done[0] <= t + LEAD_FIRST:
            forward_first(done[0])
            done[0] += 1
        while done[1] <= t + LEAD_REST:
            forward_rest(done[1])
            done[1] += 1

    def fill_copy(u, slot):
        to = d_xp if slot < SUBS else d_xm
        return rcopy(fac.at[u, slot], fac.at[u, slot], fill_send.at[u, slot], f_recv.at[u, slot], to)

    def root_fill(u):
        k, n = divmod(u, 2)
        panel = (p0_hbm, p1_hbm)[k]

        @pl.when(is_root)
        def _():
            for slot in range(2 * SUBS):
                at = pl.multiple_of(o * 1024 + slot * ROWS, ROWS)
                src = panel.at[0, pl.ds(at, ROWS), pl.ds(n * 256, 256)]
                pltpu.make_async_copy(src, fac.at[u, slot], f_recv.at[u, slot]).start()

    def wait_factor(u, *subs):
        for i in subs or range(SUBS):
            for slot in (i, SUBS + i):
                rcopy(relay.at[u, 0], fac.at[u, slot], ay_send.at[u, 0, 0], f_recv.at[u, slot], d_yp).wait_recv()
                side = dx == (3 if slot < SUBS else 1)
                send_if(jnp.logical_and(side, yh != yroot_h), lambda slot=slot: fill_copy(u, slot))

    def apply_masks(k):
        @pl.loop(0, 16)
        def _(i):
            rows = pl.ds(pl.multiple_of(i * 128, 128), 128)
            for j in range(8):
                m = jnp.full((16, 128), mask_ref[k, j, i].astype(F32), F32).astype(BF16)
                blk = inv[rows, pl.ds(j * 128, 128)].reshape(8, 16, 128)
                masked[k, rows, pl.ds(j * 128, 128)] = (blk * m[None]).reshape(128, 128)

    def transpose_panel(k):
        @pl.loop(0, 8)
        def _(i):
            at = pl.multiple_of(i * 256, 256)
            pan_t[k, :, pl.ds(at, 256)] = pan[k, pl.ds(at, 256), :].T

    def x_copy(u, j):
        zt = rem(z + OFFSETS[j], 8)
        at = pl.multiple_of(zt * 256 + (1 - o) * 128, 128)
        return rcopy(part.at[u, pl.ds(at, 128), :], xr.at[u, j], x_send.at[u, j], x_recv.at[u, j], d_core)

    def multiply(u):
        k = u // 2
        for j in range(8):
            zt = rem(z + OFFSETS[j], 8)
            rows = pl.ds(pl.multiple_of(zt * 256, 256), 256)
            val = jnp.dot(masked[k, rows, :], fac[u].reshape(1024, 256), preferred_element_type=F32) * w
            acc[u, j] = val
            part[u, rows, :] = val.astype(BF16)
        for j in range(8):
            send(lambda j=j: x_copy(u, j))

    def inner(u):
        k, n = divmod(u, 2)

        @pl.loop(0, 2)
        def _(i):
            rows = pl.ds(pl.multiple_of(i * 256, 256), 256)
            e_acc[k, rows, pl.ds(n * 256, 256)] = jnp.dot(
                pan_t[k, rows, :], part[u], preferred_element_type=F32
            )

    def z_copy(u, d, s):
        to = (d_zp, d_zm)[d]
        rows = pl.ds(0, 64) if s == 0 else pl.ds(0, 128)
        return rcopy(
            zs.at[u, d, s, rows, :], zr.at[u, d, s, rows, :], z_send.at[u, d, s], z_recv.at[u, d, s], to
        )

    def own(u, j):
        x_copy(u, j).wait_recv()
        at = pl.multiple_of(o * 128, 128)
        return acc[u, j, pl.ds(at, 128), :] + xr[u, j].astype(F32)

    def ring(u, s):
        if s == 0:
            val = own(u, 0).astype(BF16)
            zs[u, 0, 0, 0:64, :] = val[0:64]
            zs[u, 1, 0, 0:64, :] = val[64:128]
            send(lambda: z_copy(u, 0, 0))
            send(lambda: z_copy(u, 1, 0))
            return
        for d, js in ((0, PLUS), (1, MINUS)):
            val = own(u, js[s])
            z_copy(u, d, s - 1).wait_recv()
            if s == 1:
                lo, hi = val[0:64], val[64:128]
                got = zr[u, d, 0, 0:64, :].astype(F32)
                if d == 0:
                    lo = lo + got
                else:
                    hi = hi + got
                zs[u, d, 1, 0:64, :] = lo.astype(BF16)
                zs[u, d, 1, 64:128, :] = hi.astype(BF16)
            else:
                zs[u, d, s] = (val + zr[u, d, s - 1].astype(F32)).astype(BF16)
            send(lambda d=d: z_copy(u, d, s))

    def pole_copy(u):
        theirs = fin.at[u, pl.ds(pl.multiple_of((1 - p) * 64, 64), 64), :]
        return rcopy(theirs, pr.at[u], p_send.at[u], p_recv.at[u], d_pole)

    def finish(u):
        val = own(u, 7)
        z_copy(u, 0, 3).wait_recv()
        z_copy(u, 1, 3).wait_recv()
        fin[u] = val + zr[u, 0, 3].astype(F32) + zr[u, 1, 3].astype(F32)
        send(lambda: pole_copy(u))

    def pole_sum(u):
        k, n = divmod(u, 2)
        pole_copy(u).wait_recv()
        val = fin[u, pl.ds(pl.multiple_of(p * 64, 64), 64), :] + pr[u]
        dens[k, :, pl.ds(n * 256, 256)] = val

    def s2_copy(d):
        to = {"row": row, "col": rem(col + d, 16), "pole": p}
        return rcopy(sq2.at[col], sq2.at[col], s2_send.at[d], s2_recv.at[d], to)

    def s3_copy(d):
        return rcopy(sq3.at[q], sq3.at[q], s3_send.at[d], s3_recv.at[d], plane(d))

    def add_up(ref):
        tot = ref[0]
        for i in range(1, 16):
            tot = tot + ref[i]
        return tot

    def squares1():
        rows = []
        for c in range(4):
            v = dens[0, :, pl.ds(c * 128, 128)]
            rows.append(jnp.sum(v * v, axis=0, keepdims=True))
        rows.append(jnp.zeros((4, 128), F32))
        sq2[col] = jnp.concatenate(rows, axis=0)
        send_all(s2_copy, 16)

    def squares2():
        pl.loop(1, 16)(lambda d: s2_copy(d).wait_recv())
        sq3[q] = add_up(sq2)
        send_all(s3_copy, 16)

    def squares3():
        pl.loop(1, 16)(lambda d: s3_copy(d).wait_recv())
        scale[...] = jnp.sqrt(add_up(sq3) * (1.0 / 16384.0) + 1e-6)

    def scale_row():
        return jnp.concatenate([scale[c : c + 1, :] for c in range(4)], axis=1)

    def d_copy(k):
        return rcopy(dps.at[k], dpr.at[k], d_send.at[k], d_recv.at[k], d_pole)

    def diag_exchange():
        for c in ld_diag:
            c.wait()
        for k in range(2):
            dsum[k] = dslice[k, 0].astype(F32) * w
            dps[k] = dslice[k, 1].astype(F32) * w
            send(lambda k=k: d_copy(k))

    def e1_copy(k):
        return rcopy(es.at[k], er1.at[k], e1_send.at[k], e1_recv.at[k], d_core)

    def e2_copy(k, d):
        t = rem(q + d, 16)
        return rcopy(eq.at[k, t], er2.at[k, d], e2_send.at[k, d], e2_recv.at[k, d], plane(d))

    def e3_copy(k, d):
        return rcopy(e3.at[k, z], e3.at[k, z], e3_send.at[k, d], e3_recv.at[k, d], along(d))

    def e4_copy(k, d):
        return rcopy(e4.at[k], dg.at[k, o, q], e4_send.at[k, d], e4_recv.at[k, d], plane(d))

    def e5_copy(k):
        return rcopy(dg.at[k, o], dg.at[k, o], e5_send.at[k], e5_recv.at[k], d_core)

    def diag1(k):
        at = pl.multiple_of((1 - o) * 256, 256)
        es[k] = e_acc[k, pl.ds(at, 256), :].astype(BF16)
        send(lambda: e1_copy(k))

    def diag2(k):
        e1_copy(k).wait_recv()

        @pl.loop(0, 16)
        def _(t):
            at = pl.multiple_of(o * 256 + t * 16, 16)
            r = pl.ds(pl.multiple_of(t * 16, 16), 16)
            eq[k, t] = (e_acc[k, pl.ds(at, 16), :] + er1[k, r, :].astype(F32)).astype(BF16)

        send_all(lambda d: e2_copy(k, d), 16)

    def diag3(k):
        @pl.loop(1, 16)
        def _(d):
            e2_copy(k, d).wait_recv()

        tot = eq[k, q].astype(F32)
        for i in range(1, 16):
            tot = tot + er2[k, i].astype(F32)
        e3[k, z] = tot.astype(BF16)

        send_all(lambda d: e3_copy(k, d), 8)

    def diag4(k):
        @pl.loop(1, 8)
        def _(d):
            e3_copy(k, d).wait_recv()

        tot = e3[k, 0].astype(F32)
        for i in range(1, 8):
            tot = tot + e3[k, i].astype(F32)
        if k == 1:
            s = scale_row()
            base = o * 256 + q * 16
            ri = lax.broadcasted_iota(jnp.int32, (16, 512), 0) + base
            ci = lax.broadcasted_iota(jnp.int32, (16, 512), 1)
            s_full = jnp.broadcast_to(s, (16, 512))
            s_col = jnp.sum(jnp.where(ri == ci, s_full, 0.0), axis=1, keepdims=True)
            tot = tot / s_full / s_col
        d_copy(k).wait_recv()
        both = jnp.where(p == 0, dsum[k] + dpr[k], dpr[k] + dsum[k])
        val = (both - tot).astype(BF16)
        e4[k] = val
        dg[k, o, q] = val

        send_all(lambda d: e4_copy(k, d), 16)

    def diag5(k):
        @pl.loop(1, 16)
        def _(d):
            e4_copy(k, d).wait_recv()

        send(lambda: e5_copy(k))

    def diag6(k):
        e5_copy(k).wait_recv()

    for i in range(AHEAD):
        root_start(*divmod(i, SUBS))
    for u in range(UNITS):
        root_fill(u)
    tell(0, d_xp, d_xm)
    tell(3, d_zp, d_zm)
    ld_inv.wait()
    apply_masks(0)
    told(0)
    tell(1, d_yp, d_ym)
    told(3)
    tell(4, d_zp, d_zm)
    forward(-LEAD_REST)
    told(1)
    tell(2, d_yp, d_ym)
    told(4)
    tell(5, d_zp, d_zm)
    apply_masks(1)
    forward(1 - LEAD_REST)
    diag_exchange()
    told(2)
    told(5)
    for u in range(UNITS):
        forward(4 * u)
        wait_factor(u)
        forward(4 * u + 1)
        multiply(u)
        forward(4 * u + 2)
        if u == 3:
            inner(3)
            diag1(1)
        ring(u, 0)
        forward(4 * u + 3)
        if u >= 1:
            ring(u - 1, 1)
        if u >= 2:
            ring(u - 2, 2)
        if u >= 3:
            ring(u - 3, 3)
        if u == 0:
            ld_p0.wait()
            transpose_panel(0)
        if u == 1:
            ld_p1.wait()
            transpose_panel(1)
        if u < 3:
            inner(u)
        if u == 1:
            diag1(0)
    diag2(0)
    diag2(1)
    ring(1, 3)
    finish(0)
    ring(2, 2)
    ring(3, 1)
    finish(1)
    pole_sum(0)
    ring(2, 3)
    pole_sum(1)
    squares1()
    ring(3, 2)
    diag3(0)
    diag3(1)
    finish(2)
    ring(3, 3)
    squares2()
    pole_sum(2)
    diag4(0)
    finish(3)
    squares3()
    diag4(1)
    diag5(0)
    pole_sum(3)
    dens_out[0] = dens[0].astype(BF16)
    dens_out[1] = (dens[1] / scale_row()).astype(BF16)
    diag6(0)
    diag5(1)
    diag6(1)
    diag_out[...] = dg[...]

    for drain in sent:
        drain()


def body(inv_block, block_masks, panel_first, panel_second, diag_inverse, weights):
    vmem = pltpu.VMEM
    dma = pltpu.SemaphoreType.DMA
    any_spec = pl.BlockSpec(memory_space=pl.ANY)
    smem = pl.BlockSpec(memory_space=pltpu.SMEM)
    out_vmem = pl.BlockSpec(memory_space=pltpu.VMEM)
    scratch = [
        vmem((2048, 1024), BF16),
        vmem((2, 2048, 1024), BF16),
        vmem((UNITS, 2 * SUBS, ROWS, 256), BF16),
        vmem((UNITS, SUBS, ROWS, 256), BF16),
        vmem((2, 2048, 512), BF16),
        vmem((2, 512, 2048), BF16),
        vmem((UNITS, 2048, 256), BF16),
        vmem((UNITS, 8, 256, 256), F32),
        vmem((UNITS, 8, 128, 256), BF16),
        vmem((UNITS, 2, 4, 128, 256), BF16),
        vmem((UNITS, 2, 4, 128, 256), BF16),
        vmem((UNITS, 128, 256), F32),
        vmem((UNITS, 64, 256), F32),
        vmem((2, 64, 512), F32),
        vmem((2, 512, 512), F32),
        vmem((2, 256, 512), BF16),
        vmem((2, 256, 512), BF16),
        vmem((2, 16, 16, 512), BF16),
        vmem((2, 16, 16, 512), BF16),
        vmem((2, 8, 16, 512), BF16),
        vmem((2, 16, 512), BF16),
        vmem((2, 2, 16, 16, 512), BF16),
        vmem((2, 2, 16, 512), BF16),
        vmem((2, 16, 512), F32),
        vmem((2, 16, 512), F32),
        vmem((2, 16, 512), F32),
        vmem((8, 128), F32),
        vmem((16, 8, 128), F32),
        vmem((16, 8, 128), F32),
        pltpu.SemaphoreType.REGULAR((6,)),
        dma((3,)),
        dma((2, 2)),
        dma((UNITS, SUBS, 2)),
        dma((UNITS, SUBS)),
        dma((UNITS, SUBS, 2)),
        dma((UNITS, SUBS, 2)),
        dma((UNITS, 2 * SUBS)),
        dma((UNITS, 2 * SUBS)),
        dma((UNITS, 8)),
        dma((UNITS, 8)),
        dma((UNITS, 2, 4)),
        dma((UNITS, 2, 4)),
        dma((UNITS,)),
        dma((UNITS,)),
        dma((2,)),
        dma((2,)),
        dma((2, 16)),
        dma((2, 16)),
        dma((2, 8)),
        dma((2, 8)),
        dma((2, 16)),
        dma((2, 16)),
        dma((2,)),
        dma((2,)),
        dma((16,)),
        dma((16,)),
        dma((16,)),
        dma((16,)),
        dma((2,)),
        dma((2,)),
    ]
    dens, diag = pl.pallas_call(
        kernel,
        out_shape=(
            jax.ShapeDtypeStruct((2, 64, 512), BF16),
            jax.ShapeDtypeStruct((2, 2, 16, 16, 512), BF16),
        ),
        in_specs=[any_spec, smem, any_spec, any_spec, any_spec, smem],
        out_specs=(out_vmem, out_vmem),
        scratch_shapes=scratch,
        compiler_params=pltpu.CompilerParams(
            collective_id=0, has_side_effects=True, vmem_limit_bytes=60 * 1024 * 1024
        ),
    )(inv_block, block_masks.transpose(0, 2, 1), panel_first, panel_second, diag_inverse, weights)
    return dens, diag.reshape(2, 512, 512).astype(F32)


def solution(mesh):
    placed = (
        P("pole", "row", "col"),
        P(None, "row", "col"),
        P("pole", "row", None),
        P("pole", "row", None),
        P(None, "pole", None, None),
        P("pole"),
    )
    return jax.shard_map(
        body,
        mesh=mesh,
        in_specs=placed,
        out_specs=(P(None, ("row", "col", "pole"), None), P()),
        check_vma=False,
    )
```

time: 123 us -> 102 us (0.83)
  Pallas kernels: 117 us -> 97.3 us
  local copies, waits for them, and re-layouts: 2.04 us -> 0.66 us
    pallas_call x1, Pallas kernels: 117 us -> 97.3 us  [body(): pl.pallas_call(kernel, out_shape=(jax.ShapeDtypeStruct((2, 64, 512), BF16...]
    unnamed x4 -> x3, local copies, waits for them, and re-layouts: 2.04 us -> 0.66 us
where the time goes in v2:
time: 102 us
  Pallas kernels  97.3 us (95%)
  other arithmetic  2.87 us (3%)
  between operations  1.29 us (1%)
    pallas_call x1, Pallas kernels, body(): pl.pallas_call(kernel, out_shape=(jax.ShapeDtypeStruct((2, 64, 512), BF16...  97.3 us
    convert_element_type x1, other arithmetic, body(): return (dens, diag.reshape(2, 512, 512).astype(F32))  2.87 us

profile of v2, /device:TPU:1, one launch (start us, length us, event | category | flops | bytes accessed | tf_op | source)
XLA Modules:
  0.0 102.1 jit_solution(1149276726247753018)
XLA Ops:
  1.3 97.3 %shard_map.77 = (bf16[2,64,512]{2,1,0:T(8,128)(2,1)}, bf16[2,2,16,16,512]{4,3,2,1,0:T(8,128)(2,1)}) custom-call(bf16[1,2048,1024]{2,1,0:T(8,128)(2,1)} %inv_hbm.1, s32[2,8,16]{2,1,0:T(8,128)} %bitcast.4, bf16[1,2048,512]{2,1,0:T(8,128)(2,1)} %p0_hbm.1, bf16[1,2048,512]{2,1,0:T(8,128)(2,1)} %p1_hbm.1, bf16[2,1,512,512]{3,2,1,0:T(8,128)(2,1)} %diag_hbm.1, ...), custom_call_target="tpu_custom_call" | custom-call | tf_op jit(solution)/shard_map/pallas_call | solution.py:575
  98.6 0.0 copy-start
  98.6 2.9 %bitcast_convert_fusion = f32[2,512,512]{2,1,0:T(8,128)} fusion(bf16[2,2,16,16,512]{4,3,2,1,0:T(8,128)(2,1)} %get-tuple-element.5), kind=kLoop, calls=%fused_computation | loop fusion | flops 524288 | bytes 3145728 | tf_op jit(solution)/shard_map/convert_element_type | solution.py:588
  101.5 0.0 copy-done
  101.5 0.7 copy.10
Async XLA Ops:
  98.6 2.9 %copy-start = (bf16[2,64,512]{2,1,0:T(8,128)(2,1)S(1)}, bf16[2,64,512]{2,1,0:T(8,128)(2,1)}, u32[]{:S(2)}) copy-start(bf16[2,64,512]{2,1,0:T(8,128)(2,1)} %get-tuple-element.8) | copy-start | bytes 393220
